TPU v7x, 256 devices: a whole 4x4x8 slice. The times are simulated.
256 devices in a mesh: gz: 16 (over x, y), gx: 16 (over z, core).
Axes of the slice: x: 4, y: 4, z: 8, core: 2. Of those that a mesh axis runs over, the one named last changes fastest.
Arguments:
- substrate: float32 [256, 512, 1024], P('gz', 'gx'), may hold values from 0 to 1
- catalyst: float32 [256, 512, 1024], P('gz', 'gx'), may hold values from 0 to 1
- extinction: float32 [2], replicated, may hold values from 0.25 to 1
- emission: float32 [3, 2], replicated, may hold values from 0.5 to 2
Outputs:
- substrate_next: float32 [256, 512, 1024], P('gz', 'gx')
- catalyst_next: float32 [256, 512, 1024], P('gz', 'gx')
- image: float32 [4, 512, 1024], P(None, 'gx', 'gz')
All inputs are finite; a program needn't handle non-finite values.
Results may differ from a plain program's by a relative error of at most 0.00004.
Values sent between devices are 32-bit elements; how exact they have to be, the bound alone decides.
A program may use at most 64 MiB of HBM per device.

v0:
```python
import jax
import jax.numpy as jnp
from jax import lax
from jax.sharding import PartitionSpec as P

STEPS = 2


diffusion_rates = (0.16, 0.08)
feed_rate = 0.037
kill_rate = 0.06
optical_scale = 4.0


def padded_2(x, sides, width):
    edges = {}
    for axis, dim in sides:
        size, length = (lax.axis_size(axis), x.shape[dim])
        up = [(i, (i + 1) % size) for i in range(size)]
        last = lax.slice_in_dim(x, length - width, length, axis=dim)
        initial = lax.slice_in_dim(x, 0, width, axis=dim)
        edges[dim] = (
            lax.ppermute(last, axis, up),
            lax.ppermute(initial, axis, [(b, a) for a, b in up]),
        )
    done = []
    for _, dim in sides:
        low, high = edges[dim]
        around = [(width, width) if d in done else (0, 0) for d in range(x.ndim)]
        x = jnp.concatenate([jnp.pad(low, around), x, jnp.pad(high, around)], axis=dim)
        done.append(dim)
    return x


def react_padded(padded):
    centre = padded[:, 1:-1, 1:-1]
    laplace = padded[:, 2:, 1:-1] + padded[:, :-2, 1:-1]
    laplace = laplace + padded[:, 1:-1, 2:] + padded[:, 1:-1, :-2]
    laplace = laplace + jnp.roll(centre, 1, axis=3) + jnp.roll(centre, -1, axis=3)
    laplace = laplace - 6.0 * centre
    sub_old = centre[0]
    cat_old = centre[1]
    growth = sub_old * cat_old * cat_old
    sub_new = sub_old + diffusion_rates[0] * laplace[0] - growth + feed_rate * (1.0 - sub_old)
    cat_new = cat_old + diffusion_rates[1] * laplace[1] + growth - (feed_rate + kill_rate) * cat_old
    return jnp.stack([sub_new, cat_new])


def single_rim(fields):
    return padded_2(fields, (("gz", 1), ("gx", 2)), 1)


def body(substrate, catalyst, extinction, emission):
    fields = jnp.stack([substrate, catalyst])
    for step in range(STEPS):
        fields = react_padded(single_rim(fields))
    sub_final = fields[0]
    cat_final = fields[1]
    depth_total = sub_final.shape[0] * lax.axis_size("gz")
    optical = (extinction[0] * sub_final + extinction[1] * cat_final) * (
        optical_scale / depth_total
    )
    opacity = 1.0 - jnp.exp(-optical)
    before = jnp.cumsum(optical, axis=0) - optical
    weight = jnp.exp(-before) * opacity
    seen_sub = jnp.sum(weight * sub_final, axis=0)
    seen_cat = jnp.sum(weight * cat_final, axis=0)
    colour = (
        emission[:, 0, None, None] * seen_sub[None] + emission[:, 1, None, None] * seen_cat[None]
    )
    slab_depth = jnp.sum(optical, axis=0)
    stacked = jnp.concatenate([colour, slab_depth[None]], axis=0)
    gathered = lax.all_to_all(stacked[None], "gz", split_axis=3, concat_axis=0, tiled=True)
    depths = gathered[:, 3]
    ahead = jnp.cumsum(depths, axis=0) - depths
    shaded = jnp.sum(jnp.exp(-ahead)[:, None] * gathered[:, :3], axis=0)
    opaque = 1.0 - jnp.exp(-jnp.sum(depths, axis=0))
    image = jnp.concatenate([shaded, opaque[None]], axis=0)
    return (sub_final, cat_final, image)


def solution(mesh):
    placed = (P("gz", "gx", None), P("gz", "gx", None), P(), P())
    return jax.shard_map(
        body,
        mesh=mesh,
        in_specs=placed,
        out_specs=(P("gz", "gx", None), P("gz", "gx", None), P(None, "gx", "gz")),
        check_vma=False,
    )
```

profile of v0, /device:TPU:8, one launch (start us, length us, event | category | flops | bytes accessed | tf_op | source)
XLA Modules:
  0.0 77.4 jit_solution(4111072051117482208)
XLA Ops:
  0.6 1.3 %fusion.50 = (f32[2,1,32,1024]{3,2,1,0:T(8,128)S(1)}, f32[2,1,32,1024]{3,2,1,0:T(8,128)S(1)}) fusion(f32[1,16,32,1024]{3,2,1,0:T(8,128)} %bitcast.71, f32[1,16,32,1024]{3,2,1,0:T(8,128)} %bitcast.66), kind=kLoop, calls=%fused_computation.124 | loop fusion | flops 131072 | bytes 4718592 | tf_op jit(solution)/shard_map/stack | solution.py:54
  1.9 2.3 %collective-permute-start = (f32[2,1,32,1024]{3,2,1,0:T(8,128)S(1)}, f32[2,1,32,1024]{3,2,1,0:T(8,128)S(1)}, u32[]{:S(2)}, u32[]{:S(2)}) collective-permute-start(f32[2,1,32,1024]{3,2,1,0:T(8,128)S(1)} %get-tuple-element.25), channel_id=1, source_target_pairs={{16,0},{32,16},{48,32},{64,48},{80,64},{96,80},{112,96},{128,112},... | collective-permute-start | bytes 786440 | tf_op jit(solution)/shard_map/ppermute | solution.py:24
  4.2 0.2 fusion.54
  4.4 4.6 %collective-permute-start.2 = (f32[2,16,1,1024]{3,2,1,0:T(1,128)S(1)}, f32[2,16,1,1024]{3,2,1,0:T(1,128)S(1)}, u32[]{:S(2)}, u32[]{:S(2)}) collective-permute-start(f32[2,16,1,1024]{3,2,1,0:T(1,128)S(1)} %get-tuple-element.22), channel_id=1, source_target_pairs={{1,0},{2,1},{3,2},{4,3},{5,4},{6,5},{7,6},{8,7},{9,8},{10,9},{11,1... | collective-permute-start | bytes 393224 | tf_op jit(solution)/shard_map/ppermute | solution.py:24
  9.0 2.0 %fusion.5 = (f32[2,16,32,1023]{3,2,1,0:T(8,128)S(1)}, f32[2,16,32,1023]{3,2,1,0:T(8,128)S(1)}) fusion(f32[1,16,32,1024]{3,2,1,0:T(8,128)S(1)} %bitcast.73, f32[1,16,32,1024]{3,2,1,0:T(8,128)S(1)} %bitcast.68), kind=kLoop, calls=%fused_computation.39 | loop fusion | flops 2095104 | bytes 12574720 | tf_op jit(solution)/shard_map/stack | solution.py:54
  11.1 0.6 fusion.57
  11.7 0.2 fusion.46
  12.0 2.7 %collective-permute-done.3 = f32[2,16,1,1024]{3,2,1,0:T(1,128)S(1)} collective-permute-done((f32[2,16,1,1024]{3,2,1,0:T(1,128)S(1)}, f32[2,16,1,1024]{3,2,1,0:T(1,128)S(1)}, u32[]{:S(2)}, u32[]{:S(2)}) %collective-permute-start.3) | collective-permute-done | bytes 131104 | tf_op jit(solution)/shard_map/ppermute | solution.py:23
  14.7 0.6 copy-done.9
  15.5 6.4 %fusion.7 = f32[2,16,32,1024]{3,2,1,0:T(8,128)S(1)} fusion(f32[1,16,32,1024]{3,2,1,0:T(8,128)S(1)} %bitcast.70, f32[1,16,32,1024]{3,2,1,0:T(8,128)S(1)} %bitcast.75, f32[2,16,1,1024]{3,2,1,0:T(1,128)} %copy-done.9, f32[2,1,32,1024]{3,2,1,0:T(8,128)} %copy-done.4, f32[2,1,32,1024]{3,2,1,0:T(8,128)} %copy-done.5, f32[2,16,1,1024]{3,2,1,0:T(1,128)} %copy-done.8, ...), kind=kLoop, calls=%fused_computation.41 | loop fusion | flops 29360128 | bytes 17563648 | tf_op jit(solution)/shard_map/sub | solution.py:40
  21.9 1.5 %fusion.33 = (f32[16,32,1024]{2,1,0:T(8,128)S(1)}, f32[16,32,1024]{2,1,0:T(8,128)S(1)}) fusion(f32[16,32,1024]{2,1,0:T(8,128)S(1)} %copy-done, f32[2,16,32,1024]{3,2,1,0:T(8,128)S(1)} %fusion.7, f32[16,32,1024]{2,1,0:T(8,128)S(1)} %copy-done.1), kind=kLoop, calls=%fused_computation.98 | loop fusion | flops 6815744 | bytes 12582912 | tf_op jit(solution)/shard_map/sub | solution.py:45
  23.4 4.1 %collective-permute-start.4 = (f32[2,1,32,1024]{3,2,1,0:T(8,128)S(1)}, f32[2,1,32,1024]{3,2,1,0:T(8,128)S(1)}, u32[]{:S(2)}, u32[]{:S(2)}) collective-permute-start(f32[2,1,32,1024]{3,2,1,0:T(8,128)S(1)} %get-tuple-element.17), channel_id=1, source_target_pairs={{16,0},{32,16},{48,32},{64,48},{80,64},{96,80},{112,96},{128,112},... | collective-permute-start | bytes 786440 | tf_op jit(solution)/shard_map/ppermute | solution.py:24
  27.5 2.0 %fusion.1 = (f32[2,16,32,1023]{3,2,1,0:T(8,128)S(1)}, f32[2,16,32,1023]{3,2,1,0:T(8,128)S(1)}) fusion(f32[1,16,32,1024]{3,2,1,0:T(8,128)S(1)} %bitcast.62, f32[1,16,32,1024]{3,2,1,0:T(8,128)S(1)} %bitcast.57), kind=kLoop, calls=%fused_computation.35 | loop fusion | flops 2095104 | bytes 12574720 | tf_op jit(solution)/shard_map/stack | solution.py:46
  29.5 0.2 fusion.52
  29.8 3.8 %collective-permute-start.6 = (f32[2,16,1,1024]{3,2,1,0:T(1,128)S(1)}, f32[2,16,1,1024]{3,2,1,0:T(1,128)S(1)}, u32[]{:S(2)}, u32[]{:S(2)}) collective-permute-start(f32[2,16,1,1024]{3,2,1,0:T(1,128)S(1)} %get-tuple-element.14), channel_id=1, source_target_pairs={{1,0},{2,1},{3,2},{4,3},{5,4},{6,5},{7,6},{8,7},{9,8},{10,9},{11,1... | collective-permute-start | bytes 393224 | tf_op jit(solution)/shard_map/ppermute | solution.py:24
  33.6 0.2 fusion.44
  33.8 2.3 %collective-permute-done.6 = f32[2,16,1,1024]{3,2,1,0:T(1,128)S(1)} collective-permute-done((f32[2,16,1,1024]{3,2,1,0:T(1,128)S(1)}, f32[2,16,1,1024]{3,2,1,0:T(1,128)S(1)}, u32[]{:S(2)}, u32[]{:S(2)}) %collective-permute-start.6) | collective-permute-done | bytes 131104 | tf_op jit(solution)/shard_map/ppermute | solution.py:24
  36.1 3.1 %collective-permute-done.7 = f32[2,16,1,1024]{3,2,1,0:T(1,128)S(1)} collective-permute-done((f32[2,16,1,1024]{3,2,1,0:T(1,128)S(1)}, f32[2,16,1,1024]{3,2,1,0:T(1,128)S(1)}, u32[]{:S(2)}, u32[]{:S(2)}) %collective-permute-start.7) | collective-permute-done | bytes 131104 | tf_op jit(solution)/shard_map/ppermute | solution.py:23
  39.2 0.6 copy-done.11
  40.0 6.4 %fusion.3 = f32[2,16,32,1024]{3,2,1,0:T(8,128)S(1)} fusion(f32[1,16,32,1024]{3,2,1,0:T(8,128)S(1)} %bitcast.60, f32[1,16,32,1024]{3,2,1,0:T(8,128)S(1)} %bitcast.65, f32[2,16,1,1024]{3,2,1,0:T(1,128)} %copy-done.11, f32[2,1,32,1024]{3,2,1,0:T(8,128)} %copy-done.6, f32[2,1,32,1024]{3,2,1,0:T(8,128)} %copy-done.7, f32[2,16,1,1024]{3,2,1,0:T(1,128)} %copy-done.10, ...), kind=kLoop, calls=%fused_computation.37 | loop fusion | flops 29360128 | bytes 17563648 | tf_op jit(solution)/shard_map/sub | solution.py:40
  46.5 1.5 %fusion.25 = (f32[16,32,1024]{2,1,0:T(8,128)S(1)}, f32[16,32,1024]{2,1,0:T(8,128)S(1)}) fusion(f32[16,32,1024]{2,1,0:T(8,128)S(1)} %get-tuple-element.8, f32[2,16,32,1024]{3,2,1,0:T(8,128)S(1)} %fusion.3, f32[16,32,1024]{2,1,0:T(8,128)S(1)} %get-tuple-element.9), kind=kLoop, calls=%fused_computation.88 | loop fusion | flops 6815744 | bytes 12582912 | tf_op jit(solution)/shard_map/sub | solution.py:45
  48.0 2.5 %multiply_reduce_fusion.1 = (f32[32,1024]{1,0:T(8,128)S(1)}, f32[32,1024]{1,0:T(8,128)S(1)}, f32[32,1024]{1,0:T(8,128)S(1)}) fusion(f32[16,32,1024]{2,1,0:T(8,128)S(1)} %get-tuple-element.7, f32[16,32,1024]{2,1,0:T(8,128)S(1)} %get-tuple-element.6, f32[]{:T(128)} %bitcast.10, f32[]{:T(128)} %bitcast.9), kind=kOutput, calls=%fused_computation.105 | output fusion | flops 17203200 | bytes 4587528 | tf_op jit(solution)/shard_map/jit(cumsum)/reduce_window_sum | solution.py:64
  50.7 0.9 %copy.10 = f32[4,32,1024]{1,0,2:T(4,128)S(1)} copy(f32[4,32,1024]{2,1,0:T(8,128)S(1)} %pad_maximum_fusion.22) | data formatting | bytes 1048576 | tf_op jit(solution)/shard_map/concatenate | solution.py:72
  51.6 1.5 %bitcast_bitcast_fusion = f32[1024,1,4,32]{3,2,1,0:T(4,128)} fusion(f32[4,32,1024]{1,0,2:T(4,128)S(1)} %copy.10), kind=kLoop, calls=%fused_computation.137 | loop fusion | bytes 1048576
  53.0 2.8 %reshape.38 = f32[16,1,8192]{2,1,0:T(1,128)S(1)} reshape(f32[1024,1,4,32]{3,2,1,0:T(4,128)} %bitcast_bitcast_fusion) | data formatting | bytes 1048576
  55.9 16.3 %all_to_all.18 = f32[16,1,8192]{2,1,0:T(1,128)S(1)} all-to-all(f32[16,1,8192]{2,1,0:T(1,128)S(1)} %reshape.38), channel_id=1, replica_groups=mesh['gz'=16,'gx'=16] {'gz'}, dimensions={0} | all-to-all | bytes 1048576 | tf_op jit(solution)/shard_map/all_to_all | solution.py:73
  72.2 0.5 broadcast.90
  72.7 1.9 %reduce.1 = f32[16,8192]{1,0:T(8,128)S(1)} reduce(f32[16,1,8192]{2,1,0:T(1,128)S(1)} %all_to_all.18, f32[]{:T(128)} %broadcast.90), dimensions={1}, to_apply=%all_to_all.13.reduce_sub_computation | reduce | bytes 1048580 | tf_op jit(solution)/shard_map/all_to_all | solution.py:73
  74.6 1.1 %reshape.39 = f32[1024,1,4,32]{3,2,1,0:T(4,128)S(1)} reshape(f32[16,8192]{1,0:T(8,128)S(1)} %reduce.1) | data formatting | bytes 1048576
  75.7 0.8 %copy.12 = f32[1,4,32,16,64]{4,2,1,3,0:T(8,128)S(1)} copy(f32[1,4,32,16,64]{2,1,4,3,0:T(4,128)S(1)} %bitcast.76) | data formatting | bytes 1048576 | tf_op jit(solution)/shard_map/all_to_all | solution.py:73
  76.6 0.1 fusion.41
  76.7 0.6 pad_maximum_fusion.23
  (42 shorter events, 0.7 us)
Async XLA Ops:
  0.6 3.6 %copy-start.1 = (f32[16,32,1024]{2,1,0:T(8,128)S(1)}, f32[16,32,1024]{2,1,0:T(8,128)}, u32[]{:S(2)}) copy-start(f32[16,32,1024]{2,1,0:T(8,128)} %param.4) | copy-start | bytes 6291460
  0.6 3.6 %copy-start = (f32[16,32,1024]{2,1,0:T(8,128)S(1)}, f32[16,32,1024]{2,1,0:T(8,128)}, u32[]{:S(2)}) copy-start(f32[16,32,1024]{2,1,0:T(8,128)} %param.5) | copy-start | bytes 6291460
  1.9 12.7 %collective-permute-start = (f32[2,1,32,1024]{3,2,1,0:T(8,128)S(1)}, f32[2,1,32,1024]{3,2,1,0:T(8,128)S(1)}, u32[]{:S(2)}, u32[]{:S(2)}) collective-permute-start(f32[2,1,32,1024]{3,2,1,0:T(8,128)S(1)} %get-tuple-element.25), channel_id=1, source_target_pairs={{16,0},{32,16},{48,32},{64,48},{80,64},{96,80},{112,96},{128,112},... | collective-permute-start | bytes 786440 | tf_op jit(solution)/shard_map/ppermute | solution.py:24
  4.2 10.4 %collective-permute-start.1 = (f32[2,1,32,1024]{3,2,1,0:T(8,128)S(1)}, f32[2,1,32,1024]{3,2,1,0:T(8,128)S(1)}, u32[]{:S(2)}, u32[]{:S(2)}) collective-permute-start(f32[2,1,32,1024]{3,2,1,0:T(8,128)S(1)} %get-tuple-element.24), channel_id=1, source_target_pairs={{0,16},{16,32},{32,48},{48,64},{64,80},{80,96},{96,112},{112,128},... | collective-permute-start | bytes 786440 | tf_op jit(solution)/shard_map/ppermute | solution.py:23
  4.4 7.5 %collective-permute-start.2 = (f32[2,16,1,1024]{3,2,1,0:T(1,128)S(1)}, f32[2,16,1,1024]{3,2,1,0:T(1,128)S(1)}, u32[]{:S(2)}, u32[]{:S(2)}) collective-permute-start(f32[2,16,1,1024]{3,2,1,0:T(1,128)S(1)} %get-tuple-element.22), channel_id=1, source_target_pairs={{1,0},{2,1},{3,2},{4,3},{5,4},{6,5},{7,6},{8,7},{9,8},{10,9},{11,1... | collective-permute-start | bytes 393224 | tf_op jit(solution)/shard_map/ppermute | solution.py:24
  9.0 2.0 %copy-start.13 = (f32[3,2]{0,1:T(2,128)S(1)}, f32[3,2]{0,1:T(2,128)}, u32[]{:S(2)}) copy-start(f32[3,2]{0,1:T(2,128)} %param.7) | copy-start | bytes 76
  9.0 2.0 %copy-start.12 = (f32[2]{0:T(128)S(1)}, f32[2]{0:T(128)}, u32[]{:S(2)}) copy-start(f32[2]{0:T(128)} %param.6) | copy-start | bytes 28
  9.0 5.6 %collective-permute-start.3 = (f32[2,16,1,1024]{3,2,1,0:T(1,128)S(1)}, f32[2,16,1,1024]{3,2,1,0:T(1,128)S(1)}, u32[]{:S(2)}, u32[]{:S(2)}) collective-permute-start(f32[2,16,1,1024]{3,2,1,0:T(1,128)S(1)} %get-tuple-element.23), channel_id=1, source_target_pairs={{0,1},{1,2},{2,3},{3,4},{4,5},{5,6},{6,7},{7,8},{8,9},{9,10},{10,1... | collective-permute-start | bytes 393224 | tf_op jit(solution)/shard_map/ppermute | solution.py:23
  11.9 2.7 %copy-start.8 = (f32[2,16,1,1024]{3,2,1,0:T(1,128)}, f32[2,16,1,1024]{3,2,1,0:T(1,128)S(1)}, u32[]{:S(2)}) copy-start(f32[2,16,1,1024]{3,2,1,0:T(1,128)S(1)} %collective-permute-done.2) | copy-start | bytes 393220
  14.6 0.6 copy-start.9
  14.6 0.7 copy-start.4
  14.6 0.8 %copy-start.5 = (f32[2,1,32,1024]{3,2,1,0:T(8,128)}, f32[2,1,32,1024]{3,2,1,0:T(8,128)S(1)}, u32[]{:S(2)}) copy-start(f32[2,1,32,1024]{3,2,1,0:T(8,128)S(1)} %collective-permute-done.1) | copy-start | bytes 786436
  23.4 15.8 %collective-permute-start.4 = (f32[2,1,32,1024]{3,2,1,0:T(8,128)S(1)}, f32[2,1,32,1024]{3,2,1,0:T(8,128)S(1)}, u32[]{:S(2)}, u32[]{:S(2)}) collective-permute-start(f32[2,1,32,1024]{3,2,1,0:T(8,128)S(1)} %get-tuple-element.17), channel_id=1, source_target_pairs={{16,0},{32,16},{48,32},{64,48},{80,64},{96,80},{112,96},{128,112},... | collective-permute-start | bytes 786440 | tf_op jit(solution)/shard_map/ppermute | solution.py:24
  27.5 11.7 %collective-permute-start.5 = (f32[2,1,32,1024]{3,2,1,0:T(8,128)S(1)}, f32[2,1,32,1024]{3,2,1,0:T(8,128)S(1)}, u32[]{:S(2)}, u32[]{:S(2)}) collective-permute-start(f32[2,1,32,1024]{3,2,1,0:T(8,128)S(1)} %get-tuple-element.16), channel_id=1, source_target_pairs={{0,16},{16,32},{32,48},{48,64},{64,80},{80,96},{96,112},{112,128},... | collective-permute-start | bytes 786440 | tf_op jit(solution)/shard_map/ppermute | solution.py:23
  29.8 6.4 %collective-permute-start.6 = (f32[2,16,1,1024]{3,2,1,0:T(1,128)S(1)}, f32[2,16,1,1024]{3,2,1,0:T(1,128)S(1)}, u32[]{:S(2)}, u32[]{:S(2)}) collective-permute-start(f32[2,16,1,1024]{3,2,1,0:T(1,128)S(1)} %get-tuple-element.14), channel_id=1, source_target_pairs={{1,0},{2,1},{3,2},{4,3},{5,4},{6,5},{7,6},{8,7},{9,8},{10,9},{11,1... | collective-permute-start | bytes 393224 | tf_op jit(solution)/shard_map/ppermute | solution.py:24
  33.6 5.6 %collective-permute-start.7 = (f32[2,16,1,1024]{3,2,1,0:T(1,128)S(1)}, f32[2,16,1,1024]{3,2,1,0:T(1,128)S(1)}, u32[]{:S(2)}, u32[]{:S(2)}) collective-permute-start(f32[2,16,1,1024]{3,2,1,0:T(1,128)S(1)} %get-tuple-element.15), channel_id=1, source_target_pairs={{0,1},{1,2},{2,3},{3,4},{4,5},{5,6},{6,7},{7,8},{8,9},{9,10},{10,1... | collective-permute-start | bytes 393224 | tf_op jit(solution)/shard_map/ppermute | solution.py:23
  36.1 3.1 %copy-start.10 = (f32[2,16,1,1024]{3,2,1,0:T(1,128)}, f32[2,16,1,1024]{3,2,1,0:T(1,128)S(1)}, u32[]{:S(2)}) copy-start(f32[2,16,1,1024]{3,2,1,0:T(1,128)S(1)} %collective-permute-done.6) | copy-start | bytes 393220
  39.2 0.6 copy-start.11
  39.2 0.7 copy-start.6
  39.2 0.8 %copy-start.7 = (f32[2,1,32,1024]{3,2,1,0:T(8,128)}, f32[2,1,32,1024]{3,2,1,0:T(8,128)S(1)}, u32[]{:S(2)}) copy-start(f32[2,1,32,1024]{3,2,1,0:T(8,128)S(1)} %collective-permute-done.5) | copy-start | bytes 786436
  48.0 2.5 %copy-start.2 = (f32[16,32,1024]{2,1,0:T(8,128)}, f32[16,32,1024]{2,1,0:T(8,128)S(1)}, u32[]{:S(2)}) copy-start(f32[16,32,1024]{2,1,0:T(8,128)S(1)} %get-tuple-element.6) | copy-start | bytes 6291460
  48.0 2.5 %copy-start.3 = (f32[16,32,1024]{2,1,0:T(8,128)}, f32[16,32,1024]{2,1,0:T(8,128)S(1)}, u32[]{:S(2)}) copy-start(f32[16,32,1024]{2,1,0:T(8,128)S(1)} %get-tuple-element.7) | copy-start | bytes 6291460
where the time goes:
time: 77.7 us; the launch traced here: 77.4 us
  other arithmetic  27.4 us (35%)
  blocking collectives  16.3 us (21%)
  starting transfers between devices  14.8 us (19%)
  local copies, waits for them, and re-layouts  9.84 us (13%)
  waiting for transfers between devices  8.06 us (10%)
  between operations  0.94 us (1%)
    all_to_all x1, blocking collectives, body(): lax.all_to_all(stacked[None], 'gz', split_axis=3, concat_axis=0, tiled=True)  16.3 us
    ppermute x4, starting transfers between devices, padded_2(): lax.ppermute(initial, axis, [(b, a) for a, b in up])  14.8 us
    sub x2, other arithmetic, react_padded(): laplace = laplace - 6.0 * centre  12.8 us
    unnamed x31, local copies, waits for them, and re-layouts  7.01 us
    ppermute x4, waiting for transfers between devices, padded_2(): lax.ppermute(last, axis, up)  5.75 us
    another operation x4, other arithmetic, body(): fields = jnp.stack([substrate, catalyst])  3.72 us
    sub x2, other arithmetic, react_padded(): cat_old + diffusion_rates[1] * laplace[1] + growth  3.03 us
    another operation x1, other arithmetic, body(): before = jnp.cumsum(optical, axis=0) - optical  2.52 us
  transfers between devices with their start and end apart: 8, of which 3 were waited for; matrix products, arithmetic and copies ran while one was open for 7% of the time, Pallas kernels for 0%

commit v1 on v0

v1 whole, which is shorter than its diff:
```python
import functools
import math

import jax
import jax.numpy as jnp
from jax import lax
from jax.experimental import pallas as pl
from jax.experimental.pallas import tpu as pltpu
from jax.sharding import PartitionSpec as P

MESH = pl.DeviceIdType.MESH
LANES = 128
TILE = 8
OFF = 8

rate_u, rate_w = (0.16, 0.08)
feed_rate = 0.037
kill_rate = 0.06
optical_scale = 4.0
LOG2E = 1.0 / math.log(2.0)


def kernel(depth, rows, cols, n_gz, n_gx, ext_hbm, u_hbm, w_hbm,
           out_u, out_w, recv,
           u0, w0, u1, w1, acc, send, ext_ref, ext_sem, load_sems, z_send, z_recv, r_send, r_recv, a_send, a_recv):
    gz = lax.axis_index("gz")
    gx = lax.axis_index("gx")
    up, down = lax.rem(gz + 1, n_gz), lax.rem(gz + n_gz - 1, n_gz)
    right, left = lax.rem(gx + 1, n_gx), lax.rem(gx + n_gx - 1, n_gx)
    tiles = rows // TILE
    half = tiles // 2
    ncol = cols // LANES
    first, last = 1, depth
    fields0, fields1 = (u0, w0), (u1, w1)

    ext_copy = pltpu.make_async_copy(ext_hbm, ext_ref, ext_sem)
    ext_copy.start()
    for f, (src, dst) in enumerate(((u_hbm, u0), (w_hbm, w0))):
        for k, z in enumerate((0, depth - 1)):
            for c in range(ncol):
                pltpu.make_async_copy(
                    src.at[pl.ds(z, 1), :, pl.ds(c * LANES, LANES)],
                    dst.at[pl.ds(z + 1, 1), c, pl.ds(OFF, rows), :],
                    load_sems.at[0, f, k]).start()
    for f, (src, dst) in enumerate(((u_hbm, u0), (w_hbm, w0))):
        for c in range(ncol):
            pltpu.make_async_copy(
                src.at[pl.ds(1, depth - 2), :, pl.ds(c * LANES, LANES)],
                dst.at[pl.ds(2, depth - 2), c, pl.ds(OFF, rows), :],
                load_sems.at[1, f, 0]).start()

    barrier = pltpu.get_barrier_semaphore()
    for k in range(1, n_gz):
        pl.semaphore_signal(barrier, inc=1, device_id={"gz": lax.rem(gz + k, n_gz)}, device_id_type=MESH)
    for nb in (left, right):
        pl.semaphore_signal(barrier, inc=1, device_id={"gx": nb}, device_id_type=MESH)
    pl.semaphore_wait(barrier, n_gz - 1 + 2)

    def wait_local(dst, sem):
        pltpu.make_async_copy(dst, dst, sem).wait()

    for f in range(2):
        for k, z in enumerate((first, last)):
            wait_local(fields0[f].at[pl.ds(z, 1), :, pl.ds(OFF, rows), :], load_sems.at[0, f, k])

    def z_copy(step, f, side, h):
        ref = (fields0, fields1)[step][f]
        r = pl.ds(OFF + h * half * TILE, half * TILE)
        return pltpu.make_async_remote_copy(
            src_ref=ref.at[last if side == 0 else first, :, r, :],
            dst_ref=ref.at[0 if side == 0 else depth + 1, :, r, :],
            send_sem=z_send.at[step, f, side, h], recv_sem=z_recv.at[step, f, side, h],
            device_id={"gz": up if side == 0 else down}, device_id_type=MESH)

    def r_copy(step, f, side):
        ref = (fields0, fields1)[step][f]
        return pltpu.make_async_remote_copy(
            src_ref=ref.at[pl.ds(1, depth), :, pl.ds(OFF + rows - 1 if side == 0 else OFF, 1), :],
            dst_ref=ref.at[pl.ds(1, depth), :, pl.ds(OFF - 1 if side == 0 else OFF + rows, 1), :],
            send_sem=r_send.at[step, f, side], recv_sem=r_recv.at[step, f, side],
            device_id={"gx": right if side == 0 else left}, device_id_type=MESH)

    for h in range(2):
        for f in range(2):
            for side in range(2):
                z_copy(0, f, side, h).start()
    for f in range(2):
        wait_local(fields0[f].at[pl.ds(2, depth - 2), :, pl.ds(OFF, rows), :], load_sems.at[1, f, 0])
    for f in range(2):
        for side in range(2):
            r_copy(0, f, side).start()

    lane = lax.broadcasted_iota(jnp.int32, (TILE, LANES), 1)
    is_first, is_last = lane == 0, lane == LANES - 1

    def around(ref, p, t):
        r0 = OFF + t * TILE

        def at(plane, c, r):
            return ref[plane, c, pl.ds(r, TILE), :]

        def turn(x, by):
            return pltpu.roll(x, by, 1)

        centre = at(p, 0, r0)
        before = turn(at(p, ncol - 1, r0), 1)
        own_down = turn(centre, LANES - 1)
        first_down = own_down
        for c in range(ncol):
            own_up = turn(centre, 1)
            if c + 1 < ncol:
                after = at(p, c + 1, r0)
                next_down = turn(after, LANES - 1)
            else:
                after, next_down = None, first_down
            total = jnp.where(is_first, before, own_up) + jnp.where(is_last, next_down, own_down)
            total = total + (at(p, c, r0 - 1) + at(p, c, r0 + 1))
            total = total + (at(p - 1, c, r0) + at(p + 1, c, r0))
            yield centre, total
            before, own_down, centre = own_up, next_down, after

    def react(fields, p, t):
        for (u, su), (w, sw) in zip(around(fields[0], p, t), around(fields[1], p, t)):
            uw = u * w
            growth = uw * w
            u_new = u * (1.0 - 6.0 * rate_u - feed_rate) + (su * rate_u + feed_rate) - growth
            w_new = w * (1.0 - 6.0 * rate_w - feed_rate - kill_rate) + sw * rate_w + growth
            yield u_new, w_new

    def step_one(p, ts):
        for t in ts:
            for c, (un, wn) in enumerate(react(fields0, p, t)):
                u1[p, c, pl.ds(OFF + t * TILE, TILE), :] = un
                w1[p, c, pl.ds(OFF + t * TILE, TILE), :] = wn

    edge_tiles = (0, tiles - 1)
    inner_tiles = tuple(range(1, tiles - 1))

    @pl.loop(2, depth)
    def _(p):
        step_one(p, inner_tiles)

    for f in range(2):
        for side in range(2):
            r_copy(0, f, side).wait_recv()

    @pl.loop(2, depth)
    def _(p):
        step_one(p, edge_tiles)

    halves = (tuple(range(half)), tuple(range(half, tiles)))
    for h in range(2):
        for f in range(2):
            for side in range(2):
                z_copy(0, f, side, h).wait_recv()
        for p in (first, last):
            step_one(p, halves[h])
        for f in range(2):
            for side in range(2):
                z_copy(1, f, side, h).start()
    for f in range(2):
        for side in range(2):
            r_copy(1, f, side).start()

    ext_copy.wait()
    k_u = ext_ref[0] * (-optical_scale / (depth * n_gz) * LOG2E)
    k_w = ext_ref[1] * (-optical_scale / (depth * n_gz) * LOG2E)

    def step_two(p, t):
        for c, (un, wn) in enumerate(react(fields1, p, t)):
            out_u[p - 1, pl.ds(t * TILE, TILE), pl.ds(c * LANES, LANES)] = un
            out_w[p - 1, pl.ds(t * TILE, TILE), pl.ds(c * LANES, LANES)] = wn
            yield c, un, wn, jnp.exp2(un * k_u + wn * k_w)

    def march(p, ts):
        for t in ts:
            for c, un, wn, e in step_two(p, t):
                r = pl.ds(t * TILE, TILE)
                seen_t = acc[2, c, r, :]
                after = seen_t * e
                weight = seen_t - after
                acc[0, c, r, :] += weight * un
                acc[1, c, r, :] += weight * wn
                acc[2, c, r, :] = after

    acc[0] = jnp.zeros(acc.shape[1:], jnp.float32)
    acc[1] = jnp.zeros(acc.shape[1:], jnp.float32)
    acc[2] = jnp.ones(acc.shape[1:], jnp.float32)

    @pl.loop(2, depth)
    def _(p):
        march(p, inner_tiles)

    for f in range(2):
        for side in range(2):
            r_copy(1, f, side).wait_recv()

    @pl.loop(2, depth)
    def _(p):
        march(p, edge_tiles)

    low_half = lane < LANES // 2

    def a_copy(h, k):
        to = lax.rem(gz + k, n_gz)
        return pltpu.make_async_remote_copy(
            src_ref=send.at[h, to], dst_ref=recv.at[h, gz],
            send_sem=a_send.at[h, k], recv_sem=a_recv.at[h, k],
            device_id={"gz": to}, device_id_type=MESH)

    for h in range(2):
        for f in range(2):
            for side in range(2):
                z_copy(1, f, side, h).wait_recv()
        march(last, halves[h])
        for t in halves[h]:
            r = pl.ds(t * TILE, TILE)
            for c, un, wn, e in step_two(first, t):
                weight = 1.0 - e
                acc[0, c, r, :] = weight * un + e * acc[0, c, r, :]
                acc[1, c, r, :] = weight * wn + e * acc[1, c, r, :]
                acc[2, c, r, :] = e * acc[2, c, r, :]
        t0, t1 = halves[h]
        for ch in range(3):
            for c in range(ncol):
                a = acc[ch, c, pl.ds(t0 * TILE, TILE), :]
                b = acc[ch, c, pl.ds(t1 * TILE, TILE), :]
                a_turned = pltpu.roll(a, LANES // 2, 1)
                b_turned = pltpu.roll(b, LANES // 2, 1)
                send[h, 2 * c, ch] = jnp.where(low_half, a, b_turned)
                send[h, 2 * c + 1, ch] = jnp.where(low_half, a_turned, b)
        for k in range(1, n_gz):
            a_copy(h, k).start()
        recv[h, gz] = send[h, gz]

    for h in range(2):
        for k in range(1, n_gz):
            a_copy(h, k).wait_recv()
    for step in range(2):
        for f in range(2):
            for side in range(2):
                for h in range(2):
                    z_copy(step, f, side, h).wait_send()
                r_copy(step, f, side).wait_send()
    for h in range(2):
        for k in range(1, n_gz):
            a_copy(h, k).wait_send()


def finish(rows, n_gz, em_hbm, u_vmem, w_vmem, recv, out_u, out_w, out_image, em_ref, image, sems):
    copies = [pltpu.make_async_copy(em_hbm, em_ref, sems.at[0]),
              pltpu.make_async_copy(u_vmem, out_u, sems.at[1]),
              pltpu.make_async_copy(w_vmem, out_w, sems.at[2])]
    for copy in copies:
        copy.start()
    copies[0].wait()
    half = rows // TILE // 2
    for h in range(2):
        zero = jnp.zeros((TILE, LANES), jnp.float32)
        seen_u, seen_w, through = zero, zero, zero + 1.0
        for k in range(n_gz):
            seen_u = seen_u + through * recv[h, k, 0]
            seen_w = seen_w + through * recv[h, k, 1]
            through = through * recv[h, k, 2]
        for ch in range(4):
            if ch < 3:
                value = em_ref[0, ch] * seen_u + em_ref[1, ch] * seen_w
            else:
                value = 1.0 - through
            for q in range(2):
                part = pltpu.roll(value, LANES // 2, 1) if q else value
                image[ch, pl.ds((h * half + q) * TILE, TILE), :] = part[:, :LANES // 2]
    copy = pltpu.make_async_copy(image, out_image, sems.at[3])
    copy.start()
    copy.wait()
    copies[1].wait()
    copies[2].wait()


def body(substrate, catalyst, extinction, emission):
    depth, rows, cols = substrate.shape
    n_gz, n_gx = lax.axis_size("gz"), lax.axis_size("gx")
    ncol = cols // LANES
    f32 = jnp.float32
    field = pltpu.VMEM((depth + 2, ncol, rows + 2 * OFF, LANES), f32)
    sds = jax.ShapeDtypeStruct
    dma = pltpu.SemaphoreType.DMA
    any_spec, vmem_spec = pl.BlockSpec(memory_space=pl.ANY), pl.BlockSpec(memory_space=pltpu.VMEM)
    shape_of = sds(substrate.shape, f32)
    substrate = pltpu.with_memory_space_constraint(substrate, pltpu.HBM)
    catalyst = pltpu.with_memory_space_constraint(catalyst, pltpu.HBM)
    extinction = pltpu.with_memory_space_constraint(extinction, pltpu.HBM)
    emission = pltpu.with_memory_space_constraint(emission.T, pltpu.HBM)
    u_new, w_new, recv = pl.pallas_call(
        functools.partial(kernel, depth, rows, cols, n_gz, n_gx),
        name="gray_scott_rays",
        out_shape=(shape_of, shape_of, sds((2, n_gz, 3, TILE, LANES), f32)),
        in_specs=[any_spec] * 3,
        out_specs=(vmem_spec,) * 3,
        scratch_shapes=[
            field, field, field, field,
            pltpu.VMEM((3, ncol, rows, LANES), f32),
            pltpu.VMEM((2, n_gz, 3, TILE, LANES), f32),
            pltpu.SMEM((2,), f32), dma(()),
            dma((2, 2, 2)), dma((2, 2, 2, 2)), dma((2, 2, 2, 2)), dma((2, 2, 2)), dma((2, 2, 2)),
            dma((2, n_gz)), dma((2, n_gz)),
        ],
        compiler_params=pltpu.CompilerParams(
            collective_id=0, has_side_effects=True, vmem_limit_bytes=40 * 2**20),
    )(extinction, substrate, catalyst)
    return tuple(pl.pallas_call(
        functools.partial(finish, rows, n_gz),
        name="write_out",
        out_shape=(shape_of, shape_of, sds((4, rows, cols // n_gz), f32)),
        in_specs=[any_spec] + [vmem_spec] * 3,
        out_specs=(any_spec,) * 3,
        scratch_shapes=[pltpu.SMEM((2, 3), f32), pltpu.VMEM((4, rows, cols // n_gz), f32), dma((4,))],
        compiler_params=pltpu.CompilerParams(vmem_limit_bytes=8 * 2**20),
    )(emission, u_new, w_new, recv))


def solution(mesh):
    placed = (P("gz", "gx", None), P("gz", "gx", None), P(), P())
    return jax.shard_map(
        body,
        mesh=mesh,
        in_specs=placed,
        out_specs=(P("gz", "gx", None), P("gz", "gx", None), P(None, "gx", "gz")),
        check_vma=False,
    )
```

time: 77.7 us -> 33.8 us (0.44)
  Pallas kernels: 0 us -> 33.1 us
  other arithmetic: 27.4 us -> 0 us
  blocking collectives: 16.3 us -> 0 us
  starting transfers between devices: 14.8 us -> 0 us
  local copies, waits for them, and re-layouts: 9.84 us -> 0 us
  waiting for transfers between devices: 8.06 us -> 0 us
    pallas_call x0 -> x2, Pallas kernels: none -> 33.1 us  [the longest x1 31 us: body(): pl.pallas_call(functools.partial(kernel, depth, rows, cols, n_gz, n_gx),...]
    all_to_all x1 -> x0, blocking collectives: 16.3 us -> none  [body(): lax.all_to_all(stacked[None], 'gz', split_axis=3, concat_axis=0, tiled=True)]
    sub x5 -> x0, other arithmetic: 15.8 us -> none  [the longest x2 12.8 us: react_padded(): laplace = laplace - 6.0 * centre]
    ppermute x8 -> x0, starting transfers between devices: 14.8 us -> none  [the longest x4 14.8 us: padded_2(): lax.ppermute(initial, axis, [(b, a) for a, b in up])]
    another operation x10 -> x0, other arithmetic: 8.76 us -> none  [the longest x4 3.72 us: body(): fields = jnp.stack([substrate, catalyst])]
    ppermute x8 -> x0, waiting for transfers between devices: 8.06 us -> none  [the longest x4 5.75 us: padded_2(): lax.ppermute(last, axis, up)]
    unnamed x31 -> x0, local copies, waits for them, and re-layouts: 7.01 us -> none
    all_to_all x1 -> x0, other arithmetic: 1.89 us -> none  [body(): lax.all_to_all(stacked[None], 'gz', split_axis=3, concat_axis=0, tiled=True)]
  transfers between devices with their start and end apart: 8 -> 0, of which waited for: 3 -> 0; matrix products, arithmetic and copies ran while one was open for 7% -> 0% of each run, Pallas kernels for 0% -> 0%
where the time goes in v1:
time: 33.8 us; the launch traced here: 33.7 us
  Pallas kernels  33.1 us (98%)
  between operations  0.64 us (2%)
    pallas_call x1, Pallas kernels, body(): pl.pallas_call(functools.partial(kernel, depth, rows, cols, n_gz, n_gx),...  31 us
    pallas_call x1, Pallas kernels, body(): pl.pallas_call(functools.partial(finish, rows, n_gz), name='write_out', o...  2.05 us

profile of v1, /device:TPU:8, one launch (start us, length us, event | category | flops | bytes accessed | tf_op | source)
XLA Modules:
  0.0 33.7 jit_solution(1956100431479993797)
XLA Ops:
  0.6 31.0 %gray_scott_rays.1 = (f32[16,32,1024]{2,1,0:T(8,128)S(1)}, f32[16,32,1024]{2,1,0:T(8,128)S(1)}, f32[2,16,3,8,128]{4,3,2,1,0:T(8,128)S(1)}) custom-call(f32[2]{0:T(128)} %ext_hbm.1, f32[16,32,1024]{2,1,0:T(8,128)} %u_hbm.1, f32[16,32,1024]{2,1,0:T(8,128)} %w_hbm.1), custom_call_target="tpu_custom_call" | custom-call | tf_op jit(solution)/shard_map/gray_scott_rays/pallas_call | solution.py:294
  31.6 2.1 %write_out.1 = (f32[16,32,1024]{2,1,0:T(8,128)}, f32[16,32,1024]{2,1,0:T(8,128)}, f32[4,32,64]{2,1,0:T(8,128)}) custom-call(f32[2,3]{1,0:T(2,128)} %bitcast.1, f32[16,32,1024]{2,1,0:T(8,128)S(1)} %get-tuple-element.6.u_vmem, f32[16,32,1024]{2,1,0:T(8,128)S(1)} %get-tuple-element.7.w_vmem, f32[2,16,3,8,128]{4,3,2,1,0:T(8,128)S(1)} %get-tuple-element.8.recv), custom_call_target="tpu_custom_call" | custom-call | tf_op jit(solution)/shard_map/write_out/pallas_call | solution.py:311

commit v2 on v1

v2 whole, which is shorter than its diff:
```python
import functools
import math

import jax
import jax.numpy as jnp
from jax import lax
from jax.experimental import pallas as pl
from jax.experimental.pallas import tpu as pltpu
from jax.sharding import PartitionSpec as P

MESH = pl.DeviceIdType.MESH
LANES = 128
TILE = 8
OFF = 8
HALO = 2

rate_u, rate_w = (0.16, 0.08)
feed_rate = 0.037
kill_rate = 0.06
optical_scale = 4.0
LOG2E = 1.0 / math.log(2.0)


def kernel(depth, rows, cols, n_gz, n_gx, ext_hbm, u_hbm, w_hbm,
           out_u, out_w, recv,
           u0, w0, u1, w1, acc, send, row_out, row_in, corner_out, corner_in, ext_ref, ext_sem, load_sems,
           here_sems, z_send, z_recv, r_send, r_recv, c_send, c_recv, a_send, a_recv):
    gz = lax.axis_index("gz")
    gx = lax.axis_index("gx")
    tiles = rows // TILE
    ncol = cols // LANES
    first, last = HALO, HALO + depth - 1
    shells = (first - 1, last + 1)
    groups = tile_groups(tiles)
    spans_of = ((1, tiles - 2), (0, 1), (tiles - 1, 1))
    fields = ((u0, w0), (u1, w1))

    def gz_at(k):
        return {"gz": lax.rem(gz + (k + n_gz), n_gz)}

    def gx_at(k):
        return {"gx": lax.rem(gx + (k + n_gx), n_gx)}

    barrier = pltpu.get_barrier_semaphore()
    for k in (1, -1):
        pl.semaphore_signal(barrier, inc=1, device_id=gz_at(k), device_id_type=MESH)
        pl.semaphore_signal(barrier, inc=1, device_id=gx_at(k), device_id_type=MESH)

    for f, src in enumerate((u_hbm, w_hbm)):
        for k, z in enumerate((0, depth - 1)):
            for c in range(ncol):
                pltpu.make_async_copy(
                    src.at[pl.ds(z, 1), :, pl.ds(c * LANES, LANES)],
                    fields[0][f].at[pl.ds(z + HALO, 1), c, pl.ds(OFF, rows), :],
                    load_sems.at[0, f, k]).start()
    for f, src in enumerate((u_hbm, w_hbm)):
        for c in range(ncol):
            pltpu.make_async_copy(
                src.at[pl.ds(1, depth - 2), :, pl.ds(c * LANES, LANES)],
                fields[0][f].at[pl.ds(first + 1, depth - 2), c, pl.ds(OFF, rows), :],
                load_sems.at[1, f, 0]).start()
    ext_copy = pltpu.make_async_copy(ext_hbm, ext_ref, ext_sem)
    ext_copy.start()

    def wait_local(dst, sem):
        pltpu.make_async_copy(dst, dst, sem).wait()

    def z_copy(j, f, side, q):
        ref = fields[0][f]
        r = pl.ds(OFF + spans_of[q][0] * TILE, spans_of[q][1] * TILE)
        return pltpu.make_async_remote_copy(
            src_ref=ref.at[last - j if side == 0 else first + j, :, r, :],
            dst_ref=ref.at[first - 1 - j if side == 0 else last + 1 + j, :, r, :],
            send_sem=z_send.at[j, f, side, q], recv_sem=z_recv.at[j, f, side, q],
            device_id=gz_at(1 if side == 0 else -1), device_id_type=MESH)

    def corner_copy(side):
        return pltpu.make_async_remote_copy(
            src_ref=corner_out.at[side], dst_ref=corner_in.at[side],
            send_sem=c_send.at[side], recv_sem=c_recv.at[side],
            device_id=gx_at(1 if side == 0 else -1), device_id_type=MESH)

    def r_copy(step, side):
        return pltpu.make_async_remote_copy(
            src_ref=row_out.at[step, side], dst_ref=row_in.at[step, side],
            send_sem=r_send.at[step, side], recv_sem=r_recv.at[step, side],
            device_id=gx_at(1 if side == 0 else -1), device_id_type=MESH)

    def send_rows(step):
        for side in range(2):
            r = OFF + rows - 1 if side == 0 else OFF
            for f in range(2):
                for c in range(ncol):
                    row_out[step, side, f, c] = fields[step][f][pl.ds(first, depth), c, r, :]
            r_copy(step, side).start()

    def take_rows(step):
        for side in range(2):
            r = OFF - 1 if side == 0 else OFF + rows
            r_copy(step, side).wait_recv()
            for f in range(2):
                for c in range(ncol):
                    fields[step][f][pl.ds(first, depth), c, r, :] = row_in[step, side, f, c]

    def send_corners():
        for side in range(2):
            r = OFF + rows - 1 if side == 0 else OFF
            for f in range(2):
                for k in range(2):
                    corner_out[side, f, k] = fields[0][f][shells[k], pl.ds(0, ncol), r, :]
            corner_copy(side).start()

    def take_corners():
        for side in range(2):
            r = OFF - 1 if side == 0 else OFF + rows
            corner_copy(side).wait_recv()
            for f in range(2):
                for k in range(2):
                    fields[0][f][shells[k], pl.ds(0, ncol), r, :] = corner_in[side, f, k]

    def each_z(step, g, act):
        for q in ((0,), (1, 2))[g]:
            for f in range(2):
                for side in range(2):
                    act(z_copy(step, f, side, q))

    pl.semaphore_wait(barrier, 4)
    spans = []
    while (1 << len(spans)) < n_gz // 2:
        spans.append(1 << len(spans))

    def tell(i):
        if i < len(spans):
            for k in (spans[i], -spans[i]):
                pl.semaphore_signal(here_sems.at[i], inc=1, device_id=gz_at(k), device_id_type=MESH)

    def hear(i):
        if i < len(spans):
            pl.semaphore_wait(here_sems.at[i], 2)

    for f in range(2):
        for k, z in enumerate((first, last)):
            wait_local(fields[0][f].at[pl.ds(z, 1), :, pl.ds(OFF, rows), :], load_sems.at[0, f, k])
    each_z(0, 0, lambda copy: copy.start())
    tell(0)
    for f in range(2):
        wait_local(fields[0][f].at[pl.ds(first + 1, depth - 2), :, pl.ds(OFF, rows), :], load_sems.at[1, f, 0])
    send_rows(0)
    each_z(0, 1, lambda copy: copy.start())
    each_z(1, 0, lambda copy: copy.start())

    lane = lax.broadcasted_iota(jnp.int32, (TILE, LANES), 1)
    is_first, is_last = lane == 0, lane == LANES - 1

    def around(ref, p, t):
        r0 = OFF + t * TILE

        def at(plane, c, r):
            return ref[plane, c, pl.ds(r, TILE), :]

        def turn(x, by):
            return pltpu.roll(x, by, 1)

        centre = at(p, 0, r0)
        before = turn(at(p, ncol - 1, r0), 1)
        own_down = turn(centre, LANES - 1)
        first_down = own_down
        for c in range(ncol):
            own_up = turn(centre, 1)
            if c + 1 < ncol:
                after = at(p, c + 1, r0)
                next_down = turn(after, LANES - 1)
            else:
                after, next_down = None, first_down
            total = jnp.where(is_first, before, own_up) + jnp.where(is_last, next_down, own_down)
            total = total + (at(p, c, r0 - 1) + at(p, c, r0 + 1))
            total = total + (at(p - 1, c, r0) + at(p + 1, c, r0))
            yield centre, total
            before, own_down, centre = own_up, next_down, after

    def react(step, p, t):
        for (u, su), (w, sw) in zip(around(fields[step][0], p, t), around(fields[step][1], p, t)):
            uw = u * w
            growth = uw * w
            u_new = u * (1.0 - 6.0 * rate_u - feed_rate) + (su * rate_u + feed_rate) - growth
            w_new = w * (1.0 - 6.0 * rate_w - feed_rate - kill_rate) + sw * rate_w + growth
            yield u_new, w_new

    def step_one(p, ts):
        for t in ts:
            for c, (un, wn) in enumerate(react(0, p, t)):
                u1[p, c, pl.ds(OFF + t * TILE, TILE), :] = un
                w1[p, c, pl.ds(OFF + t * TILE, TILE), :] = wn

    def inside(act):
        @pl.loop(first + 1, last)
        def _(p):
            act(p)

    inner, edges = groups

    inside(lambda p: step_one(p, inner))
    hear(0)
    tell(1)
    take_rows(0)
    inside(lambda p: step_one(p, edges))
    hear(1)
    tell(2)
    for g, group in enumerate(groups):
        each_z(0, g, lambda copy: copy.wait_recv())
        for p in (first, last):
            step_one(p, group)
    send_corners()
    send_rows(1)
    each_z(1, 1, lambda copy: copy.start())

    ext_copy.wait()
    k_u = ext_ref[0] * (-optical_scale / (depth * n_gz) * LOG2E)
    k_w = ext_ref[1] * (-optical_scale / (depth * n_gz) * LOG2E)

    def step_two(p, t):
        for c, (un, wn) in enumerate(react(1, p, t)):
            out_u[p - first, pl.ds(t * TILE, TILE), pl.ds(c * LANES, LANES)] = un
            out_w[p - first, pl.ds(t * TILE, TILE), pl.ds(c * LANES, LANES)] = wn
            yield c, un, wn, jnp.exp2(un * k_u + wn * k_w)

    def march(p, ts):
        for t in ts:
            r = pl.ds(t * TILE, TILE)
            for c, un, wn, e in step_two(p, t):
                through = acc[2, c, r, :]
                after = through * e
                weight = through - after
                acc[0, c, r, :] += weight * un
                acc[1, c, r, :] += weight * wn
                acc[2, c, r, :] = after

    acc[0] = jnp.zeros(acc.shape[1:], jnp.float32)
    acc[1] = jnp.zeros(acc.shape[1:], jnp.float32)
    acc[2] = jnp.ones(acc.shape[1:], jnp.float32)

    inside(lambda p: march(p, inner))
    hear(2)

    low_half = lane < LANES // 2

    side = 4 if n_gz % 4 == 0 else 1
    turns = [(i, j) for i in range(n_gz // side) for j in range(side) if i or j]
    turns.sort(key=lambda t: -(min(t[0], n_gz // side - t[0]) + min(t[1], side - t[1])))

    def a_copy(h, i, j):
        fast = lax.rem(gz, side)
        to = lax.rem(gz - fast + i * side, n_gz) + lax.rem(fast + j, side)
        return pltpu.make_async_remote_copy(
            src_ref=send.at[h, to], dst_ref=recv.at[h, gz],
            send_sem=a_send.at[h], recv_sem=a_recv.at[h],
            device_id={"gz": to}, device_id_type=MESH)

    def a_all(h):
        rest = pl.ds(0, n_gz - 1)
        return pltpu.make_async_remote_copy(
            src_ref=send.at[h, rest], dst_ref=recv.at[h, rest],
            send_sem=a_send.at[h], recv_sem=a_recv.at[h],
            device_id=gz_at(1), device_id_type=MESH)

    for h, group in enumerate(groups):
        if h == 1:
            take_rows(1)
            inside(lambda p: march(p, edges))
            take_corners()
        each_z(1, h, lambda copy: copy.wait_recv())
        for p in shells:
            step_one(p, group)
        march(last, group)
        for t in group:
            r = pl.ds(t * TILE, TILE)
            for c, un, wn, e in step_two(first, t):
                weight = 1.0 - e
                acc[0, c, r, :] = weight * un + e * acc[0, c, r, :]
                acc[1, c, r, :] = weight * wn + e * acc[1, c, r, :]
                acc[2, c, r, :] = e * acc[2, c, r, :]
        t0, t1 = group
        for ch in range(3):
            for c in range(ncol):
                a = acc[ch, c, pl.ds(t0 * TILE, TILE), :]
                b = acc[ch, c, pl.ds(t1 * TILE, TILE), :]
                send[h, 2 * c, ch] = jnp.where(low_half, a, pltpu.roll(b, LANES // 2, 1))
                send[h, 2 * c + 1, ch] = jnp.where(low_half, pltpu.roll(a, LANES // 2, 1), b)
        for i, j in turns:
            a_copy(h, i, j).start()
        recv[h, gz] = send[h, gz]

    for step in range(2):
        for side in range(2):
            r_copy(step, side).wait_send()
            if step:
                corner_copy(side).wait_send()
        for h in range(2):
            each_z(step, h, lambda copy: copy.wait_send())
    for h in range(2):
        a_all(h).wait_send()
    for h in range(2):
        a_all(h).wait_recv()


def tile_groups(tiles):
    return tuple(range(1, tiles - 1)), (0, tiles - 1)


def finish(rows, n_gz, em_hbm, u_vmem, w_vmem, recv, out_u, out_w, out_image, em_ref, image, sems):
    copies = [pltpu.make_async_copy(em_hbm, em_ref, sems.at[0]),
              pltpu.make_async_copy(u_vmem, out_u, sems.at[1]),
              pltpu.make_async_copy(w_vmem, out_w, sems.at[2])]
    for copy in copies:
        copy.start()
    copies[0].wait()
    for h, group in enumerate(tile_groups(rows // TILE)):
        zero = jnp.zeros((TILE, LANES), jnp.float32)
        seen_u, seen_w, through = zero, zero, zero + 1.0
        for k in range(n_gz):
            seen_u = seen_u + through * recv[h, k, 0]
            seen_w = seen_w + through * recv[h, k, 1]
            through = through * recv[h, k, 2]
        for ch in range(4):
            if ch < 3:
                value = em_ref[0, ch] * seen_u + em_ref[1, ch] * seen_w
            else:
                value = 1.0 - through
            for q in range(2):
                part = pltpu.roll(value, LANES // 2, 1) if q else value
                image[ch, pl.ds(group[q] * TILE, TILE), :] = part[:, :LANES // 2]
    copy = pltpu.make_async_copy(image, out_image, sems.at[3])
    copy.start()
    copy.wait()
    copies[1].wait()
    copies[2].wait()


def body(substrate, catalyst, extinction, emission):
    depth, rows, cols = substrate.shape
    n_gz, n_gx = lax.axis_size("gz"), lax.axis_size("gx")
    ncol = cols // LANES
    f32 = jnp.float32
    field = pltpu.VMEM((depth + 2 * HALO, ncol, rows + 2 * OFF, LANES), f32)
    sds = jax.ShapeDtypeStruct
    dma = pltpu.SemaphoreType.DMA
    any_spec, vmem_spec = pl.BlockSpec(memory_space=pl.ANY), pl.BlockSpec(memory_space=pltpu.VMEM)
    shape_of = sds(substrate.shape, f32)
    substrate = pltpu.with_memory_space_constraint(substrate, pltpu.HBM)
    catalyst = pltpu.with_memory_space_constraint(catalyst, pltpu.HBM)
    extinction = pltpu.with_memory_space_constraint(extinction, pltpu.HBM)
    emission = pltpu.with_memory_space_constraint(emission.T, pltpu.HBM)
    u_new, w_new, recv = pl.pallas_call(
        functools.partial(kernel, depth, rows, cols, n_gz, n_gx),
        name="gray_scott_rays",
        out_shape=(shape_of, shape_of, sds((2, n_gz, 3, TILE, LANES), f32)),
        in_specs=[any_spec] * 3,
        out_specs=(vmem_spec,) * 3,
        scratch_shapes=[
            field, field, field, field,
            pltpu.VMEM((3, ncol, rows, LANES), f32),
            pltpu.VMEM((2, n_gz, 3, TILE, LANES), f32),
            pltpu.VMEM((2, 2, 2, ncol, depth, LANES), f32),
            pltpu.VMEM((2, 2, 2, ncol, depth, LANES), f32),
            pltpu.VMEM((2, 2, 2, ncol, LANES), f32),
            pltpu.VMEM((2, 2, 2, ncol, LANES), f32),
            pltpu.SMEM((2,), f32), dma(()), dma((2, 2, 2)), pltpu.SemaphoreType.REGULAR((3,)),
            dma((2, 2, 2, 3)), dma((2, 2, 2, 3)), dma((2, 2)), dma((2, 2)), dma((2,)), dma((2,)),
            dma((2,)), dma((2,)),
        ],
        compiler_params=pltpu.CompilerParams(
            collective_id=0, has_side_effects=True, vmem_limit_bytes=40 * 2**20),
    )(extinction, substrate, catalyst)
    return tuple(pl.pallas_call(
        functools.partial(finish, rows, n_gz),
        name="write_out",
        out_shape=(shape_of, shape_of, sds((4, rows, cols // n_gz), f32)),
        in_specs=[any_spec] + [vmem_spec] * 3,
        out_specs=(any_spec,) * 3,
        scratch_shapes=[pltpu.SMEM((2, 3), f32), pltpu.VMEM((4, rows, cols // n_gz), f32), dma((4,))],
        compiler_params=pltpu.CompilerParams(vmem_limit_bytes=8 * 2**20),
    )(emission, u_new, w_new, recv))


def solution(mesh):
    placed = (P("gz", "gx", None), P("gz", "gx", None), P(), P())
    return jax.shard_map(
        body,
        mesh=mesh,
        in_specs=placed,
        out_specs=(P("gz", "gx", None), P("gz", "gx", None), P(None, "gx", "gz")),
        check_vma=False,
    )
```

time: 33.8 us -> 31.9 us (0.944)
  Pallas kernels: 33.1 us -> 30.9 us
    pallas_call x1, Pallas kernels: 31 us -> 28.8 us  [body(): pl.pallas_call(functools.partial(kernel, depth, rows, cols, n_gz, n_gx),...]
where the time goes in v2:
time: 31.9 us; the launch traced here: 31.5 us
  Pallas kernels  30.9 us (97%)
  between operations  0.64 us (2%)
    pallas_call x1, Pallas kernels, body(): pl.pallas_call(functools.partial(kernel, depth, rows, cols, n_gz, n_gx),...  28.8 us
    pallas_call x1, Pallas kernels, body(): pl.pallas_call(functools.partial(finish, rows, n_gz), name='write_out', o...  2.05 us

profile of v2, /device:TPU:8, one launch (start us, length us, event | category | flops | bytes accessed | tf_op | source)
XLA Modules:
  0.0 31.5 jit_solution(10992789631025587499)
XLA Ops:
  0.6 28.8 %gray_scott_rays.1 = (f32[16,32,1024]{2,1,0:T(8,128)S(1)}, f32[16,32,1024]{2,1,0:T(8,128)S(1)}, f32[2,16,3,8,128]{4,3,2,1,0:T(8,128)S(1)}) custom-call(f32[2]{0:T(128)} %ext_hbm.1, f32[16,32,1024]{2,1,0:T(8,128)} %u_hbm.1, f32[16,32,1024]{2,1,0:T(8,128)} %w_hbm.1), custom_call_target="tpu_custom_call" | custom-call | tf_op jit(solution)/shard_map/gray_scott_rays/pallas_call | solution.py:353
  29.5 2.1 %write_out.1 = (f32[16,32,1024]{2,1,0:T(8,128)}, f32[16,32,1024]{2,1,0:T(8,128)}, f32[4,32,64]{2,1,0:T(8,128)}) custom-call(f32[2,3]{1,0:T(2,128)} %bitcast.1, f32[16,32,1024]{2,1,0:T(8,128)S(1)} %get-tuple-element.6.u_vmem, f32[16,32,1024]{2,1,0:T(8,128)S(1)} %get-tuple-element.7.w_vmem, f32[2,16,3,8,128]{4,3,2,1,0:T(8,128)S(1)} %get-tuple-element.8.recv), custom_call_target="tpu_custom_call" | custom-call | tf_op jit(solution)/shard_map/write_out/pallas_call | solution.py:374

commit v3 on v2

--- a/solution.py
+++ b/solution.py
@@ -10,6 +10,7 @@
 
 MESH = pl.DeviceIdType.MESH
 LANES = 128
+RANK = (0, 1, 0, 1, 0, 2, 1, 0, 1, 2, 1, 0, 1, 0, 2, 1)
 TILE = 8
 OFF = 8
 HALO = 2
@@ -41,10 +42,11 @@
     def gx_at(k):
         return {"gx": lax.rem(gx + (k + n_gx), n_gx)}
 
+    rank = RANK if len(RANK) == n_gx else range(n_gx)
+
     barrier = pltpu.get_barrier_semaphore()
     for k in (1, -1):
         pl.semaphore_signal(barrier, inc=1, device_id=gz_at(k), device_id_type=MESH)
-        pl.semaphore_signal(barrier, inc=1, device_id=gx_at(k), device_id_type=MESH)
 
     for f, src in enumerate((u_hbm, w_hbm)):
         for k, z in enumerate((0, depth - 1)):
@@ -124,7 +126,12 @@
                 for side in range(2):
                     act(z_copy(step, f, side, q))
 
-    pl.semaphore_wait(barrier, 4)
+    lower = sum(
+        (jnp.where(gx == i, 1, 0) for i in range(n_gx) for k in (1, -1) if rank[(i + k) % n_gx] < rank[i]),
+        jnp.int32(0))
+    pl.semaphore_wait(barrier, 2 + lower)
+    for k in (1, -1):
+        pl.semaphore_signal(barrier, inc=1, device_id=gx_at(k), device_id_type=MESH)
     spans = []
     while (1 << len(spans)) < n_gz // 2:
         spans.append(1 << len(spans))
@@ -145,9 +152,9 @@
     tell(0)
     for f in range(2):
         wait_local(fields[0][f].at[pl.ds(first + 1, depth - 2), :, pl.ds(OFF, rows), :], load_sems.at[1, f, 0])
-    send_rows(0)
     each_z(0, 1, lambda copy: copy.start())
     each_z(1, 0, lambda copy: copy.start())
+    each_z(1, 1, lambda copy: copy.start())
 
     lane = lax.broadcasted_iota(jnp.int32, (TILE, LANES), 1)
     is_first, is_last = lane == 0, lane == LANES - 1
@@ -200,20 +207,26 @@
     inner, edges = groups
 
     inside(lambda p: step_one(p, inner))
+
+    @pl.when(lower < 2)
+    def _():
+        pl.semaphore_wait(barrier, 2 - lower)
+
+    send_rows(0)
     hear(0)
     tell(1)
+    each_z(0, 0, lambda copy: copy.wait_recv())
+    for p in (first, last):
+        step_one(p, inner)
     take_rows(0)
     inside(lambda p: step_one(p, edges))
     hear(1)
     tell(2)
-    for g, group in enumerate(groups):
-        each_z(0, g, lambda copy: copy.wait_recv())
-        for p in (first, last):
-            step_one(p, group)
+    each_z(0, 1, lambda copy: copy.wait_recv())
+    for p in (first, last):
+        step_one(p, edges)
     send_corners()
     send_rows(1)
-    each_z(1, 1, lambda copy: copy.start())
-
     ext_copy.wait()
     k_u = ext_ref[0] * (-optical_scale / (depth * n_gz) * LOG2E)
     k_w = ext_ref[1] * (-optical_scale / (depth * n_gz) * LOG2E)

time: 31.9 us -> 31.6 us (level)
  no operation moved by 1% of the time
where the time goes in v3:
time: 31.6 us; the launch traced here: 31.4 us
  Pallas kernels  30.8 us (97%)
  between operations  0.64 us (2%)
    pallas_call x1, Pallas kernels, body(): pl.pallas_call(functools.partial(kernel, depth, rows, cols, n_gz, n_gx),...  28.7 us
    pallas_call x1, Pallas kernels, body(): pl.pallas_call(functools.partial(finish, rows, n_gz), name='write_out', o...  2.05 us

profile of v3, /device:TPU:8, one launch (start us, length us, event | category | flops | bytes accessed | tf_op | source)
XLA Modules:
  0.0 31.4 jit_solution(15507213633855783109)
XLA Ops:
  0.6 28.7 %gray_scott_rays.1 = (f32[16,32,1024]{2,1,0:T(8,128)S(1)}, f32[16,32,1024]{2,1,0:T(8,128)S(1)}, f32[2,16,3,8,128]{4,3,2,1,0:T(8,128)S(1)}) custom-call(f32[2]{0:T(128)} %ext_hbm.1, f32[16,32,1024]{2,1,0:T(8,128)} %u_hbm.1, f32[16,32,1024]{2,1,0:T(8,128)} %w_hbm.1), custom_call_target="tpu_custom_call" | custom-call | tf_op jit(solution)/shard_map/gray_scott_rays/pallas_call | solution.py:366
  29.4 2.1 %write_out.1 = (f32[16,32,1024]{2,1,0:T(8,128)}, f32[16,32,1024]{2,1,0:T(8,128)}, f32[4,32,64]{2,1,0:T(8,128)}) custom-call(f32[2,3]{1,0:T(2,128)} %bitcast.1, f32[16,32,1024]{2,1,0:T(8,128)S(1)} %get-tuple-element.6.u_vmem, f32[16,32,1024]{2,1,0:T(8,128)S(1)} %get-tuple-element.7.w_vmem, f32[2,16,3,8,128]{4,3,2,1,0:T(8,128)S(1)} %get-tuple-element.8.recv), custom_call_target="tpu_custom_call" | custom-call | tf_op jit(solution)/shard_map/write_out/pallas_call | solution.py:387

commit v4 on v3

--- a/solution.py
+++ b/solution.py
@@ -200,7 +200,7 @@
                 w1[p, c, pl.ds(OFF + t * TILE, TILE), :] = wn
 
     def inside(act):
-        @pl.loop(first + 1, last)
+        @pl.loop(first + 1, last, unroll=2)
         def _(p):
             act(p)
 

time: 31.6 us -> 31 us (0.981)
  Pallas kernels: 30.8 us -> 30.1 us
    pallas_call x1, Pallas kernels: 28.7 us -> 28 us  [body(): pl.pallas_call(functools.partial(kernel, depth, rows, cols, n_gz, n_gx),...]
where the time goes in v4:
time: 31 us; the launch traced here: 30.7 us
  Pallas kernels  30.1 us (97%)
  between operations  0.64 us (2%)
    pallas_call x1, Pallas kernels, body(): pl.pallas_call(functools.partial(kernel, depth, rows, cols, n_gz, n_gx),...  28 us
    pallas_call x1, Pallas kernels, body(): pl.pallas_call(functools.partial(finish, rows, n_gz), name='write_out', o...  2.05 us

profile of v4, /device:TPU:8, one launch (start us, length us, event | category | flops | bytes accessed | tf_op | source)
XLA Modules:
  0.0 30.7 jit_solution(9335092722452144289)
XLA Ops:
  0.6 28.0 %gray_scott_rays.1 = (f32[16,32,1024]{2,1,0:T(8,128)S(1)}, f32[16,32,1024]{2,1,0:T(8,128)S(1)}, f32[2,16,3,8,128]{4,3,2,1,0:T(8,128)S(1)}) custom-call(f32[2]{0:T(128)} %ext_hbm.1, f32[16,32,1024]{2,1,0:T(8,128)} %u_hbm.1, f32[16,32,1024]{2,1,0:T(8,128)} %w_hbm.1), custom_call_target="tpu_custom_call" | custom-call | tf_op jit(solution)/shard_map/gray_scott_rays/pallas_call | solution.py:366
  28.7 2.1 %write_out.1 = (f32[16,32,1024]{2,1,0:T(8,128)}, f32[16,32,1024]{2,1,0:T(8,128)}, f32[4,32,64]{2,1,0:T(8,128)}) custom-call(f32[2,3]{1,0:T(2,128)} %bitcast.1, f32[16,32,1024]{2,1,0:T(8,128)S(1)} %get-tuple-element.6.u_vmem, f32[16,32,1024]{2,1,0:T(8,128)S(1)} %get-tuple-element.7.w_vmem, f32[2,16,3,8,128]{4,3,2,1,0:T(8,128)S(1)} %get-tuple-element.8.recv), custom_call_target="tpu_custom_call" | custom-call | tf_op jit(solution)/shard_map/write_out/pallas_call | solution.py:387
